TPU v7x, 512 devices: a whole 4x8x8 slice. The times are simulated.
512 devices in a mesh: section: 16 (over y, z_hi), dp: 32 (over z_lo, x, core).
Axes of the slice: x: 4, y: 8, z: 8 (z_hi: 2, z_lo: 4; z = z_hi * 4 + z_lo), core: 2. Of those that a mesh axis runs over, the one named last changes fastest.
Arguments:
- section_input: bfloat16 [6, 768, 3072], P(None, 'dp'), may hold values from -6 to 6
- loss_grad: bfloat16 [6, 768, 3072], P(None, 'dp'), may hold values from -6 to 6
- norm_gain: float32 [16, 3072], P('section'), may hold values from 0.1 to 1.9
- channel_order: int32 [16, 3072], P('section'), may hold values from 0 to 3071, each once within a row
- right_factor: bfloat16 [16, 3072, 768], P('section', 'dp'), may hold values from -0.15625 to 0.15625
- left_factor: bfloat16 [16, 3072, 768], P('section', 'dp'), may hold values from -0.15625 to 0.15625
Outputs:
- section_output: bfloat16 [16, 6, 768, 3072], P('section', None, 'dp')
- left_grad: float32 [16, 768, 768], P('section', 'dp')
Inputs may be any that keep to these rules, and one draw needn't show every extreme that they name: `channel_order`: each layer's row is a permutation of the 3072 channels.
All inputs are finite; a program needn't handle non-finite values.
Results may differ from a plain program's by a relative error of at most 0.03.
Values may be sent and summed in bfloat16 or wider, within the bound.
A program may use at most 64 MiB of HBM per device.

v0:
```python
import jax
import jax.numpy as jnp
from jax import lax
from jax.sharding import PartitionSpec as P

epsilon = 1e-05


def shifted(array, axis, by):
    peers = lax.axis_size(axis)
    pairs = [(i, i + by) for i in range(peers) if 0 <= i + by < peers]
    return lax.ppermute(array, axis, pairs)


def block_apply(values, factor):
    row_count = values.shape[0]
    block_size = factor.shape[1]
    block_count = factor.shape[0] // block_size
    result = jnp.einsum(
        "rnk,nkj->rnj",
        values.reshape(row_count, block_count, block_size),
        factor.reshape(block_count, block_size, block_size),
        preferred_element_type=jnp.float32,
    )
    return result.reshape(row_count, block_count * block_size)


def block_transposed(values, factor):
    row_count = values.shape[0]
    block_size = factor.shape[1]
    block_count = factor.shape[0] // block_size
    result = jnp.einsum(
        "rnj,nkj->rnk",
        values.reshape(row_count, block_count, block_size),
        factor.reshape(block_count, block_size, block_size),
        preferred_element_type=jnp.float32,
    )
    return result.reshape(row_count, block_count * block_size)


def inverse_norm(inputs):
    wide_in = inputs.astype(jnp.float32)
    return (wide_in, lax.rsqrt(jnp.mean(wide_in * wide_in, axis=-1, keepdims=True) + epsilon))


def layer_forward(inputs, gain_row, shuffle, right_full, left_full):
    wide_in, inverse_rms = inverse_norm(inputs)
    normed = (wide_in * inverse_rms * gain_row).astype(jnp.bfloat16)
    mixed = block_apply(normed, right_full).astype(jnp.bfloat16)
    permuted = jnp.take(mixed, shuffle, axis=1)
    output = (wide_in + block_apply(permuted, left_full)).astype(jnp.bfloat16)
    return (output, permuted)


def layer_backward(inputs, upstream, gain_row, inverse, right_full, left_full):
    wide_in, inverse_rms = inverse_norm(inputs)
    through = block_transposed(upstream, left_full).astype(jnp.bfloat16)
    before = jnp.take(through, inverse, axis=1)
    scaled = block_transposed(before, right_full) * gain_row
    cubed = inverse_rms * inverse_rms * inverse_rms
    grad_input = (
        upstream.astype(jnp.float32)
        + inverse_rms * scaled
        - wide_in * cubed * jnp.mean(scaled * wide_in, axis=-1, keepdims=True)
    )
    return grad_input.astype(jnp.bfloat16)


def store_slot(buffer, batch_slot, is_valid, new_value):
    old_value = lax.dynamic_index_in_dim(buffer, batch_slot, 0, keepdims=False)
    return lax.dynamic_update_index_in_dim(
        buffer, jnp.where(is_valid, new_value, old_value), batch_slot, 0
    )


def per_device(section_input, loss_grad, norm_gain, channel_order, right_factor, left_factor):
    sections = lax.axis_size("section")
    section_index = lax.axis_index("section")
    micro_count, row_count, channels = section_input.shape
    block_size = right_factor.shape[2]
    right_full, left_full = (
        lax.all_gather(right_factor[0], "dp", axis=0, tiled=True),
        lax.all_gather(left_factor[0], "dp", axis=0, tiled=True),
    )
    gain_row = norm_gain[0]
    shuffle = channel_order[0]
    inverse = (
        jnp.zeros((channels,), jnp.int32).at[shuffle].set(jnp.arange(channels, dtype=jnp.int32))
    )
    empty_buf = jnp.zeros((micro_count, row_count, channels), jnp.bfloat16)
    empty_head = jnp.zeros((micro_count, row_count, block_size), jnp.bfloat16)
    empty_rows = jnp.zeros((row_count, channels), jnp.bfloat16)
    is_first = section_index == 0
    is_last = section_index == sections - 1

    def run_forward(inputs):
        output, permuted = layer_forward(inputs, gain_row, shuffle, right_full, left_full)
        return (output, permuted[:, :block_size])

    def skip_forward(inputs):
        return (jnp.zeros_like(inputs), jnp.zeros((row_count, block_size), jnp.bfloat16))

    def run_backward(operands):
        return layer_backward(operands[0], operands[1], gain_row, inverse, right_full, left_full)

    def skip_backward(operands):
        return jnp.zeros_like(operands[1])

    def forward_part(forward_state, step_num):
        incoming, saved_in, saved_permuted, outputs = forward_state
        batch_pos = step_num - section_index
        is_valid = (batch_pos >= 0) & (batch_pos < micro_count)
        batch_slot = jnp.clip(batch_pos, 0, micro_count - 1)
        inputs = jnp.where(
            is_first,
            lax.dynamic_index_in_dim(section_input, batch_slot, 0, keepdims=False),
            incoming,
        )
        output, permuted_head = lax.cond(is_valid, run_forward, skip_forward, inputs)
        saved_in = store_slot(saved_in, batch_slot, is_valid, inputs)
        saved_permuted = store_slot(saved_permuted, batch_slot, is_valid, permuted_head)
        outputs = store_slot(outputs, batch_slot, is_valid, output)
        passed = shifted(output, "section", 1)
        return (passed, saved_in, saved_permuted, outputs)

    def backward_part(backward_state, saved_in, step_num, lag_steps):
        incoming, saved_upstream = backward_state
        batch_pos = step_num - lag_steps + section_index
        is_valid = (batch_pos >= 0) & (batch_pos < micro_count)
        batch_slot = jnp.clip(batch_pos, 0, micro_count - 1)
        upstream = jnp.where(
            is_last, lax.dynamic_index_in_dim(loss_grad, batch_slot, 0, keepdims=False), incoming
        )
        inputs = lax.dynamic_index_in_dim(saved_in, batch_slot, 0, keepdims=False)
        grad_input = lax.cond(is_valid, run_backward, skip_backward, (inputs, upstream))
        saved_upstream = store_slot(saved_upstream, batch_slot, is_valid, upstream[:, :block_size])
        passed = shifted(grad_input, "section", -1)
        return (passed, saved_upstream)

    forward_init = (empty_rows, empty_buf, empty_head, empty_buf)
    backward_init = (empty_rows, empty_head)

    def forward_step(forward_state, step_num):
        return (forward_part(forward_state, step_num), None)

    forward_state, ignored = lax.scan(
        forward_step, forward_init, jnp.arange(sections + micro_count - 1, dtype=jnp.int32)
    )

    def backward_step(backward_state, step_num):
        return (backward_part(backward_state, forward_state[1], step_num, sections - 1), None)

    backward_state, ignored = lax.scan(
        backward_step, backward_init, jnp.arange(sections + micro_count - 1, dtype=jnp.int32)
    )
    row_total = micro_count * row_count
    left_rows = forward_state[2].reshape(row_total, block_size)
    right_rows = backward_state[1].reshape(row_total, block_size)
    left_term = lax.dot_general(
        left_rows, right_rows, (((0,), (0,)), ((), ())), preferred_element_type=jnp.float32
    )
    left_term = left_term.astype(jnp.bfloat16)
    left_total = lax.psum(left_term, "dp").astype(jnp.float32)
    share_rows = block_size // lax.axis_size("dp")
    first_row = lax.axis_index("dp") * share_rows
    left_shard = lax.dynamic_slice_in_dim(left_total, first_row, share_rows, 0)
    return (forward_state[3][None], left_shard[None])


def solution(mesh):
    in_specs = (
        P(None, "dp", None),
        P(None, "dp", None),
        P("section", None),
        P("section", None),
        P("section", "dp", None),
        P("section", "dp", None),
    )
    out_specs = (P("section", None, "dp", None), P("section", "dp", None))
    return jax.shard_map(
        per_device, mesh=mesh, in_specs=in_specs, out_specs=out_specs, check_vma=False
    )
```

profile of v0, /device:TPU:8, one launch (start us, length us, event | category | flops | bytes accessed | tf_op | source)
XLA Modules:
  0.0 1806.3 jit_solution(8007107845714510100)
XLA Ops:
  9.5 11.8 scatter_custom_fusion
  21.3 59.8 %all-gather.5.cloned.1.call-done = bf16[1,3072,768]{2,1,0:T(8,128)(2,1)} async-done(((bf16[1,96,768]{2,1,0:T(8,128)(2,1)}), bf16[1,3072,768]{2,1,0:T(8,128)(2,1)}) %all-gather.5.cloned.1.call-update) | async-done | bytes 4718608 | tf_op jit(solution)/shard_map/all_gather | solution.py:82
  81.0 67.5 %all-gather.7.cloned.1.call-done = bf16[1,3072,768]{2,1,0:T(8,128)(2,1)} async-done(((bf16[1,96,768]{2,1,0:T(8,128)(2,1)}), bf16[1,3072,768]{2,1,0:T(8,128)(2,1)}) %all-gather.7.cloned.1.call-update) | async-done | bytes 4718608 | tf_op jit(solution)/shard_map/all_gather | solution.py:83
  150.8 549.9 %while.30 = (s32[]{:T(128)}, bf16[24,3072]{1,0:T(8,128)(2,1)S(1)}, bf16[6,24,3072]{2,1,0:T(8,128)(2,1)S(1)}, bf16[6,24,768]{1,2,0:T(8,128)(2,1)}, bf16[6,24,3072...) while((s32[]{:T(128)}, bf16[24,3072]{1,0:T(8,128)(2,1)S(1)}, ...), condition=%wide.region_4.6_spmd, body=%wide.region_0.5_spmd.sunk | while | flops 227721248 | bytes 15824611 | solution.py:146
  179.9 32.0 %collective-permute-done = bf16[24,3072]{1,0:T(8,128)(2,1)S(1)} collective-permute-done((bf16[24,3072]{1,0:T(8,128)(2,1)S(1)}, bf16[24,3072]{1,0:T(8,128)(2,1)S(1)}, u32[]{:S(2)}, u32[]{:S(2)}) %collective-permute-start) | collective-permute-done | bytes 147488 | tf_op jit(solution)/shard_map/while/body/eval_jaxpr/ppermute | solution.py:12
  214.2 19.4 %conditional.4 = (bf16[24,3072]{1,0:T(8,128)(2,1)S(1)}, bf16[24,768]{0,1:T(8,128)(2,1)S(1)}) conditional(s32[]{:T(128)} %convert_element_type.97, () %tuple.71, (bf16[24,3072]{1,0:T(8,128)(2,1)S(1)}, f32[1,3072]{1,0:T(1,128)S(1)}, bf16[3072,768]{1,0:T(8,128)(2,1)}, s32[3072]{0:T(1024)S(1)}, bf16[3072,768]{1,0:T(8,128)(2,1)}) %tuple.72), branch_computations={%region_1.1_spmd, %region_2.4_spmd} | conditional | flops 227481632 | bytes 13120912 | solution.py:119
  218.0 9.2 gather_fusion.1
  249.5 19.4 %conditional.4 = (bf16[24,3072]{1,0:T(8,128)(2,1)S(1)}, bf16[24,768]{0,1:T(8,128)(2,1)S(1)}) conditional(s32[]{:T(128)} %convert_element_type.97, () %tuple.71, (bf16[24,3072]{1,0:T(8,128)(2,1)S(1)}, f32[1,3072]{1,0:T(1,128)S(1)}, bf16[3072,768]{1,0:T(8,128)(2,1)}, s32[3072]{0:T(1024)S(1)}, bf16[3072,768]{1,0:T(8,128)(2,1)}) %tuple.72), branch_computations={%region_1.1_spmd, %region_2.4_spmd} | conditional | flops 227481632 | bytes 13120912 | solution.py:119
  253.3 9.2 gather_fusion.1
  284.7 19.4 %conditional.4 = (bf16[24,3072]{1,0:T(8,128)(2,1)S(1)}, bf16[24,768]{0,1:T(8,128)(2,1)S(1)}) conditional(s32[]{:T(128)} %convert_element_type.97, () %tuple.71, (bf16[24,3072]{1,0:T(8,128)(2,1)S(1)}, f32[1,3072]{1,0:T(1,128)S(1)}, bf16[3072,768]{1,0:T(8,128)(2,1)}, s32[3072]{0:T(1024)S(1)}, bf16[3072,768]{1,0:T(8,128)(2,1)}) %tuple.72), branch_computations={%region_1.1_spmd, %region_2.4_spmd} | conditional | flops 227481632 | bytes 13120912 | solution.py:119
  288.5 9.2 gather_fusion.1
  319.9 19.4 %conditional.4 = (bf16[24,3072]{1,0:T(8,128)(2,1)S(1)}, bf16[24,768]{0,1:T(8,128)(2,1)S(1)}) conditional(s32[]{:T(128)} %convert_element_type.97, () %tuple.71, (bf16[24,3072]{1,0:T(8,128)(2,1)S(1)}, f32[1,3072]{1,0:T(1,128)S(1)}, bf16[3072,768]{1,0:T(8,128)(2,1)}, s32[3072]{0:T(1024)S(1)}, bf16[3072,768]{1,0:T(8,128)(2,1)}) %tuple.72), branch_computations={%region_1.1_spmd, %region_2.4_spmd} | conditional | flops 227481632 | bytes 13120912 | solution.py:119
  323.6 9.2 gather_fusion.1
  354.8 19.4 %conditional.4 = (bf16[24,3072]{1,0:T(8,128)(2,1)S(1)}, bf16[24,768]{0,1:T(8,128)(2,1)S(1)}) conditional(s32[]{:T(128)} %convert_element_type.97, () %tuple.71, (bf16[24,3072]{1,0:T(8,128)(2,1)S(1)}, f32[1,3072]{1,0:T(1,128)S(1)}, bf16[3072,768]{1,0:T(8,128)(2,1)}, s32[3072]{0:T(1024)S(1)}, bf16[3072,768]{1,0:T(8,128)(2,1)}) %tuple.72), branch_computations={%region_1.1_spmd, %region_2.4_spmd} | conditional | flops 227481632 | bytes 13120912 | solution.py:119
  358.5 9.2 gather_fusion.1
  389.7 19.4 %conditional.4 = (bf16[24,3072]{1,0:T(8,128)(2,1)S(1)}, bf16[24,768]{0,1:T(8,128)(2,1)S(1)}) conditional(s32[]{:T(128)} %convert_element_type.97, () %tuple.71, (bf16[24,3072]{1,0:T(8,128)(2,1)S(1)}, f32[1,3072]{1,0:T(1,128)S(1)}, bf16[3072,768]{1,0:T(8,128)(2,1)}, s32[3072]{0:T(1024)S(1)}, bf16[3072,768]{1,0:T(8,128)(2,1)}) %tuple.72), branch_computations={%region_1.1_spmd, %region_2.4_spmd} | conditional | flops 227481632 | bytes 13120912 | solution.py:119
  393.4 9.2 gather_fusion.1
  424.8 18.8 %collective-permute-start = (bf16[24,3072]{1,0:T(8,128)(2,1)S(1)}, bf16[24,3072]{1,0:T(8,128)(2,1)S(1)}, u32[]{:S(2)}, u32[]{:S(2)}) collective-permute-start(bf16[24,3072]{1,0:T(8,128)(2,1)S(1)} %get-tuple-element.514), channel_id=1, source_target_pairs={{0,32},{32,64},{64,96},{96,128},{128,160},{160,192},{192,224},{224... | collective-permute-start | bytes 442376 | tf_op jit(solution)/shard_map/while/body/eval_jaxpr/ppermute | solution.py:12
  464.8 23.6 %collective-permute-start = (bf16[24,3072]{1,0:T(8,128)(2,1)S(1)}, bf16[24,3072]{1,0:T(8,128)(2,1)S(1)}, u32[]{:S(2)}, u32[]{:S(2)}) collective-permute-start(bf16[24,3072]{1,0:T(8,128)(2,1)S(1)} %get-tuple-element.514), channel_id=1, source_target_pairs={{0,32},{32,64},{64,96},{96,128},{128,160},{160,192},{192,224},{224... | collective-permute-start | bytes 442376 | tf_op jit(solution)/shard_map/while/body/eval_jaxpr/ppermute | solution.py:12
  494.1 10.5 collective-permute-start
  511.9 18.4 %collective-permute-start = (bf16[24,3072]{1,0:T(8,128)(2,1)S(1)}, bf16[24,3072]{1,0:T(8,128)(2,1)S(1)}, u32[]{:S(2)}, u32[]{:S(2)}) collective-permute-start(bf16[24,3072]{1,0:T(8,128)(2,1)S(1)} %get-tuple-element.514), channel_id=1, source_target_pairs={{0,32},{32,64},{64,96},{96,128},{128,160},{160,192},{192,224},{224... | collective-permute-start | bytes 442376 | tf_op jit(solution)/shard_map/while/body/eval_jaxpr/ppermute | solution.py:12
  536.0 9.1 collective-permute-start
  553.8 19.5 %collective-permute-start = (bf16[24,3072]{1,0:T(8,128)(2,1)S(1)}, bf16[24,3072]{1,0:T(8,128)(2,1)S(1)}, u32[]{:S(2)}, u32[]{:S(2)}) collective-permute-start(bf16[24,3072]{1,0:T(8,128)(2,1)S(1)} %get-tuple-element.514), channel_id=1, source_target_pairs={{0,32},{32,64},{64,96},{96,128},{128,160},{160,192},{192,224},{224... | collective-permute-start | bytes 442376 | tf_op jit(solution)/shard_map/while/body/eval_jaxpr/ppermute | solution.py:12
  579.0 13.0 collective-permute-start
  598.5 15.1 collective-permute-start
  619.3 8.5 collective-permute-start
  634.4 22.8 %collective-permute-start = (bf16[24,3072]{1,0:T(8,128)(2,1)S(1)}, bf16[24,3072]{1,0:T(8,128)(2,1)S(1)}, u32[]{:S(2)}, u32[]{:S(2)}) collective-permute-start(bf16[24,3072]{1,0:T(8,128)(2,1)S(1)} %get-tuple-element.514), channel_id=1, source_target_pairs={{0,32},{32,64},{64,96},{96,128},{128,160},{160,192},{192,224},{224... | collective-permute-start | bytes 442376 | tf_op jit(solution)/shard_map/while/body/eval_jaxpr/ppermute | solution.py:12
  662.9 14.1 collective-permute-start
  682.7 14.7 collective-permute-start
  700.8 798.9 %while.31 = (s32[]{:T(128)}, bf16[24,3072]{1,0:T(8,128)(2,1)S(1)}, bf16[6,24,768]{2,1,0:T(8,128)(2,1)S(1)}, s32[21]{0:T(128)S(1)}, s32[]{:T(128)}, /*index=5*/pr...) while((s32[]{:T(128)}, bf16[24,3072]{1,0:T(8,128)(2,1)S(1)}, ...), condition=%wide.region_11.13_spmd, body=%wide.region_6.12_spmd.sunk | while | flops 227942480 | bytes 15207745 | solution.py:153
  705.0 15.1 collective-permute-done.1
  724.3 18.8 %collective-permute-done.1 = bf16[24,3072]{1,0:T(8,128)(2,1)S(1)} collective-permute-done((bf16[24,3072]{1,0:T(8,128)(2,1)S(1)}, bf16[24,3072]{1,0:T(8,128)(2,1)S(1)}, u32[]{:S(2)}, u32[]{:S(2)}) %collective-permute-start.1) | collective-permute-done | bytes 147488 | tf_op jit(solution)/shard_map/while/body/eval_jaxpr/ppermute | solution.py:12
  747.3 13.6 collective-permute-done.1
  765.1 17.5 collective-permute-done.1
  786.9 14.6 collective-permute-done.1
  805.6 19.8 %collective-permute-done.1 = bf16[24,3072]{1,0:T(8,128)(2,1)S(1)} collective-permute-done((bf16[24,3072]{1,0:T(8,128)(2,1)S(1)}, bf16[24,3072]{1,0:T(8,128)(2,1)S(1)}, u32[]{:S(2)}, u32[]{:S(2)}) %collective-permute-start.1) | collective-permute-done | bytes 147488 | tf_op jit(solution)/shard_map/while/body/eval_jaxpr/ppermute | solution.py:12
  829.6 12.6 collective-permute-done.1
  846.4 19.2 %collective-permute-done.1 = bf16[24,3072]{1,0:T(8,128)(2,1)S(1)} collective-permute-done((bf16[24,3072]{1,0:T(8,128)(2,1)S(1)}, bf16[24,3072]{1,0:T(8,128)(2,1)S(1)}, u32[]{:S(2)}, u32[]{:S(2)}) %collective-permute-start.1) | collective-permute-done | bytes 147488 | tf_op jit(solution)/shard_map/while/body/eval_jaxpr/ppermute | solution.py:12
  869.8 16.2 collective-permute-done.1
  890.3 18.2 %collective-permute-done.1 = bf16[24,3072]{1,0:T(8,128)(2,1)S(1)} collective-permute-done((bf16[24,3072]{1,0:T(8,128)(2,1)S(1)}, bf16[24,3072]{1,0:T(8,128)(2,1)S(1)}, u32[]{:S(2)}, u32[]{:S(2)}) %collective-permute-start.1) | collective-permute-done | bytes 147488 | tf_op jit(solution)/shard_map/while/body/eval_jaxpr/ppermute | solution.py:12
  912.6 16.7 collective-permute-done.1
  933.5 15.5 collective-permute-done.1
  953.2 274.6 %collective-permute-done.1 = bf16[24,3072]{1,0:T(8,128)(2,1)S(1)} collective-permute-done((bf16[24,3072]{1,0:T(8,128)(2,1)S(1)}, bf16[24,3072]{1,0:T(8,128)(2,1)S(1)}, u32[]{:S(2)}, u32[]{:S(2)}) %collective-permute-start.1) | collective-permute-done | bytes 147488 | tf_op jit(solution)/shard_map/while/body/eval_jaxpr/ppermute | solution.py:12
  1229.9 20.4 %conditional.5 = (bf16[24,3072]{1,0:T(8,128)(2,1)S(1)}) conditional(s32[]{:T(128)} %convert_element_type.98, () %tuple.74, (bf16[24,3072]{1,0:T(8,128)(2,1)S(1)}, bf16[6,24,3072]{2,1,0:T(8,128)(2,1)S(1)}, s32[]{:T(128)}, bf16[3072,768]{1,0:T(8,128)(2,1)}, s32[3072]{0:T(1024)S(1)}, /*index=5*/bf16[3072,768]{1,0:T(8,128)(2,1)}, ...), branch_computations={%region_7.8_spmd, %region_8.11_spmd} | conditional | flops 227850304 | bytes 13990880 | solution.py:135
  1234.2 9.2 gather_fusion
  1252.3 14.6 collective-permute-done.1
  1269.1 20.4 %conditional.5 = (bf16[24,3072]{1,0:T(8,128)(2,1)S(1)}) conditional(s32[]{:T(128)} %convert_element_type.98, () %tuple.74, (bf16[24,3072]{1,0:T(8,128)(2,1)S(1)}, bf16[6,24,3072]{2,1,0:T(8,128)(2,1)S(1)}, s32[]{:T(128)}, bf16[3072,768]{1,0:T(8,128)(2,1)}, s32[3072]{0:T(1024)S(1)}, /*index=5*/bf16[3072,768]{1,0:T(8,128)(2,1)}, ...), branch_computations={%region_7.8_spmd, %region_8.11_spmd} | conditional | flops 227850304 | bytes 13990880 | solution.py:135
  1273.3 9.2 gather_fusion
  1291.5 19.0 %collective-permute-done.1 = bf16[24,3072]{1,0:T(8,128)(2,1)S(1)} collective-permute-done((bf16[24,3072]{1,0:T(8,128)(2,1)S(1)}, bf16[24,3072]{1,0:T(8,128)(2,1)S(1)}, u32[]{:S(2)}, u32[]{:S(2)}) %collective-permute-start.1) | collective-permute-done | bytes 147488 | tf_op jit(solution)/shard_map/while/body/eval_jaxpr/ppermute | solution.py:12
  1312.6 20.4 %conditional.5 = (bf16[24,3072]{1,0:T(8,128)(2,1)S(1)}) conditional(s32[]{:T(128)} %convert_element_type.98, () %tuple.74, (bf16[24,3072]{1,0:T(8,128)(2,1)S(1)}, bf16[6,24,3072]{2,1,0:T(8,128)(2,1)S(1)}, s32[]{:T(128)}, bf16[3072,768]{1,0:T(8,128)(2,1)}, s32[3072]{0:T(1024)S(1)}, /*index=5*/bf16[3072,768]{1,0:T(8,128)(2,1)}, ...), branch_computations={%region_7.8_spmd, %region_8.11_spmd} | conditional | flops 227850304 | bytes 13990880 | solution.py:135
  1316.9 9.2 gather_fusion
  1335.0 12.4 collective-permute-done.1
  1349.5 20.4 %conditional.5 = (bf16[24,3072]{1,0:T(8,128)(2,1)S(1)}) conditional(s32[]{:T(128)} %convert_element_type.98, () %tuple.74, (bf16[24,3072]{1,0:T(8,128)(2,1)S(1)}, bf16[6,24,3072]{2,1,0:T(8,128)(2,1)S(1)}, s32[]{:T(128)}, bf16[3072,768]{1,0:T(8,128)(2,1)}, s32[3072]{0:T(1024)S(1)}, /*index=5*/bf16[3072,768]{1,0:T(8,128)(2,1)}, ...), branch_computations={%region_7.8_spmd, %region_8.11_spmd} | conditional | flops 227850304 | bytes 13990880 | solution.py:135
  1353.8 9.2 gather_fusion
  1371.9 11.6 collective-permute-done.1
  1385.7 20.4 %conditional.5 = (bf16[24,3072]{1,0:T(8,128)(2,1)S(1)}) conditional(s32[]{:T(128)} %convert_element_type.98, () %tuple.74, (bf16[24,3072]{1,0:T(8,128)(2,1)S(1)}, bf16[6,24,3072]{2,1,0:T(8,128)(2,1)S(1)}, s32[]{:T(128)}, bf16[3072,768]{1,0:T(8,128)(2,1)}, s32[3072]{0:T(1024)S(1)}, /*index=5*/bf16[3072,768]{1,0:T(8,128)(2,1)}, ...), branch_computations={%region_7.8_spmd, %region_8.11_spmd} | conditional | flops 227850304 | bytes 13990880 | solution.py:135
  1390.0 9.2 gather_fusion
  1408.1 15.3 collective-permute-done.1
  1425.6 20.4 %conditional.5 = (bf16[24,3072]{1,0:T(8,128)(2,1)S(1)}) conditional(s32[]{:T(128)} %convert_element_type.98, () %tuple.74, (bf16[24,3072]{1,0:T(8,128)(2,1)S(1)}, bf16[6,24,3072]{2,1,0:T(8,128)(2,1)S(1)}, s32[]{:T(128)}, bf16[3072,768]{1,0:T(8,128)(2,1)}, s32[3072]{0:T(1024)S(1)}, /*index=5*/bf16[3072,768]{1,0:T(8,128)(2,1)}, ...), branch_computations={%region_7.8_spmd, %region_8.11_spmd} | conditional | flops 227850304 | bytes 13990880 | solution.py:135
  1429.8 9.2 gather_fusion
  1447.9 9.0 collective-permute-done.1
  1459.1 23.2 %collective-permute-start.1 = (bf16[24,3072]{1,0:T(8,128)(2,1)S(1)}, bf16[24,3072]{1,0:T(8,128)(2,1)S(1)}, u32[]{:S(2)}, u32[]{:S(2)}) collective-permute-start(bf16[24,3072]{1,0:T(8,128)(2,1)S(1)} %get-tuple-element.635), channel_id=1, source_target_pairs={{32,0},{64,32},{96,64},{128,96},{160,128},{192,160},{224,192},{256... | collective-permute-start | bytes 442376 | tf_op jit(solution)/shard_map/while/body/eval_jaxpr/ppermute | solution.py:12
  1487.2 9.2 collective-permute-start.1
  1502.6 295.8 %all-reduce.2.cloned.1.call-done = bf16[768,768]{1,0:T(8,128)(2,1)} async-done(((bf16[768,768]{1,0:T(8,128)(2,1)}), bf16[768,768]{1,0:T(8,128)(2,1)}) %all-reduce.2.cloned.1.call-update) | async-done | bytes 1179664 | tf_op jit(solution)/shard_map/psum | solution.py:163
  (546 shorter events, 411.6 us)
Async XLA Ops:
  7.2 143.7 %copy-start.1 = (s32[1,3072]{1,0:T(1,128)S(1)}, s32[1,3072]{1,0:T(1,128)}, u32[]{:S(2)}) copy-start(s32[1,3072]{1,0:T(1,128)} %param.19) | copy-start | bytes 36868
  7.2 143.7 %copy-start = (f32[1,3072]{1,0:T(1,128)S(1)}, f32[1,3072]{1,0:T(1,128)}, u32[]{:S(2)}) copy-start(f32[1,3072]{1,0:T(1,128)} %param.18) | copy-start | bytes 36868
  7.2 73.9 %all-gather.5.cloned.1.call-start = ((), (), s32[]{:S(2)}) async-start(), calls=%async_computation.1 | async-start | bytes 4866048 | tf_op jit(solution)/shard_map/all_gather | solution.py:82
  7.9 140.6 %all-gather.7.cloned.1.call-start = ((), (), s32[]{:S(2)}) async-start(), calls=%async_computation.2 | async-start | bytes 4866048 | tf_op jit(solution)/shard_map/all_gather | solution.py:83
  8.7 1789.7 %all-reduce.2.cloned.1.call-start = ((), (), s32[]{:S(2)}) async-start(), calls=%async_computation | async-start | bytes 2359296 | tf_op jit(solution)/shard_map/psum | solution.py:163
  153.2 14.9 collective-permute-start
  170.5 41.5 %collective-permute-start = (bf16[24,3072]{1,0:T(8,128)(2,1)S(1)}, bf16[24,3072]{1,0:T(8,128)(2,1)S(1)}, u32[]{:S(2)}, u32[]{:S(2)}) collective-permute-start(bf16[24,3072]{1,0:T(8,128)(2,1)S(1)} %get-tuple-element.514), channel_id=1, source_target_pairs={{0,32},{32,64},{64,96},{96,128},{128,160},{160,192},{192,224},{224... | collective-permute-start | bytes 442376 | tf_op jit(solution)/shard_map/while/body/eval_jaxpr/ppermute | solution.py:12
  233.6 13.7 collective-permute-start
  268.9 13.5 collective-permute-start
  304.0 13.5 collective-permute-start
  339.2 13.3 collective-permute-start
  374.1 13.3 collective-permute-start
  409.0 13.5 collective-permute-start
  424.8 22.2 %collective-permute-start = (bf16[24,3072]{1,0:T(8,128)(2,1)S(1)}, bf16[24,3072]{1,0:T(8,128)(2,1)S(1)}, u32[]{:S(2)}, u32[]{:S(2)}) collective-permute-start(bf16[24,3072]{1,0:T(8,128)(2,1)S(1)} %get-tuple-element.514), channel_id=1, source_target_pairs={{0,32},{32,64},{64,96},{96,128},{128,160},{160,192},{192,224},{224... | collective-permute-start | bytes 442376 | tf_op jit(solution)/shard_map/while/body/eval_jaxpr/ppermute | solution.py:12
  449.3 13.1 collective-permute-start
  464.8 27.0 %collective-permute-start = (bf16[24,3072]{1,0:T(8,128)(2,1)S(1)}, bf16[24,3072]{1,0:T(8,128)(2,1)S(1)}, u32[]{:S(2)}, u32[]{:S(2)}) collective-permute-start(bf16[24,3072]{1,0:T(8,128)(2,1)S(1)} %get-tuple-element.514), channel_id=1, source_target_pairs={{0,32},{32,64},{64,96},{96,128},{128,160},{160,192},{192,224},{224... | collective-permute-start | bytes 442376 | tf_op jit(solution)/shard_map/while/body/eval_jaxpr/ppermute | solution.py:12
  494.1 15.4 collective-permute-start
  511.9 21.7 %collective-permute-start = (bf16[24,3072]{1,0:T(8,128)(2,1)S(1)}, bf16[24,3072]{1,0:T(8,128)(2,1)S(1)}, u32[]{:S(2)}, u32[]{:S(2)}) collective-permute-start(bf16[24,3072]{1,0:T(8,128)(2,1)S(1)} %get-tuple-element.514), channel_id=1, source_target_pairs={{0,32},{32,64},{64,96},{96,128},{128,160},{160,192},{192,224},{224... | collective-permute-start | bytes 442376 | tf_op jit(solution)/shard_map/while/body/eval_jaxpr/ppermute | solution.py:12
  536.0 15.5 collective-permute-start
  553.8 22.8 %collective-permute-start = (bf16[24,3072]{1,0:T(8,128)(2,1)S(1)}, bf16[24,3072]{1,0:T(8,128)(2,1)S(1)}, u32[]{:S(2)}, u32[]{:S(2)}) collective-permute-start(bf16[24,3072]{1,0:T(8,128)(2,1)S(1)} %get-tuple-element.514), channel_id=1, source_target_pairs={{0,32},{32,64},{64,96},{96,128},{128,160},{160,192},{192,224},{224... | collective-permute-start | bytes 442376 | tf_op jit(solution)/shard_map/while/body/eval_jaxpr/ppermute | solution.py:12
  579.0 17.1 collective-permute-start
  598.5 18.4 %collective-permute-start = (bf16[24,3072]{1,0:T(8,128)(2,1)S(1)}, bf16[24,3072]{1,0:T(8,128)(2,1)S(1)}, u32[]{:S(2)}, u32[]{:S(2)}) collective-permute-start(bf16[24,3072]{1,0:T(8,128)(2,1)S(1)} %get-tuple-element.514), channel_id=1, source_target_pairs={{0,32},{32,64},{64,96},{96,128},{128,160},{160,192},{192,224},{224... | collective-permute-start | bytes 442376 | tf_op jit(solution)/shard_map/while/body/eval_jaxpr/ppermute | solution.py:12
  619.3 12.8 collective-permute-start
  634.4 26.2 %collective-permute-start = (bf16[24,3072]{1,0:T(8,128)(2,1)S(1)}, bf16[24,3072]{1,0:T(8,128)(2,1)S(1)}, u32[]{:S(2)}, u32[]{:S(2)}) collective-permute-start(bf16[24,3072]{1,0:T(8,128)(2,1)S(1)} %get-tuple-element.514), channel_id=1, source_target_pairs={{0,32},{32,64},{64,96},{96,128},{128,160},{160,192},{192,224},{224... | collective-permute-start | bytes 442376 | tf_op jit(solution)/shard_map/while/body/eval_jaxpr/ppermute | solution.py:12
  662.9 17.4 collective-permute-start
  682.7 18.1 %collective-permute-start = (bf16[24,3072]{1,0:T(8,128)(2,1)S(1)}, bf16[24,3072]{1,0:T(8,128)(2,1)S(1)}, u32[]{:S(2)}, u32[]{:S(2)}) collective-permute-start(bf16[24,3072]{1,0:T(8,128)(2,1)S(1)} %get-tuple-element.514), channel_id=1, source_target_pairs={{0,32},{32,64},{64,96},{96,128},{128,160},{160,192},{192,224},{224... | collective-permute-start | bytes 442376 | tf_op jit(solution)/shard_map/while/body/eval_jaxpr/ppermute | solution.py:12
  703.0 17.1 collective-permute-start.1
  722.4 20.7 %collective-permute-start.1 = (bf16[24,3072]{1,0:T(8,128)(2,1)S(1)}, bf16[24,3072]{1,0:T(8,128)(2,1)S(1)}, u32[]{:S(2)}, u32[]{:S(2)}) collective-permute-start(bf16[24,3072]{1,0:T(8,128)(2,1)S(1)} %get-tuple-element.635), channel_id=1, source_target_pairs={{32,0},{64,32},{96,64},{128,96},{160,128},{192,160},{224,192},{256... | collective-permute-start | bytes 442376 | tf_op jit(solution)/shard_map/while/body/eval_jaxpr/ppermute | solution.py:12
  745.3 15.6 collective-permute-start.1
  763.2 19.5 %collective-permute-start.1 = (bf16[24,3072]{1,0:T(8,128)(2,1)S(1)}, bf16[24,3072]{1,0:T(8,128)(2,1)S(1)}, u32[]{:S(2)}, u32[]{:S(2)}) collective-permute-start(bf16[24,3072]{1,0:T(8,128)(2,1)S(1)} %get-tuple-element.635), channel_id=1, source_target_pairs={{32,0},{64,32},{96,64},{128,96},{160,128},{192,160},{224,192},{256... | collective-permute-start | bytes 442376 | tf_op jit(solution)/shard_map/while/body/eval_jaxpr/ppermute | solution.py:12
  784.9 16.5 collective-permute-start.1
  803.6 21.7 %collective-permute-start.1 = (bf16[24,3072]{1,0:T(8,128)(2,1)S(1)}, bf16[24,3072]{1,0:T(8,128)(2,1)S(1)}, u32[]{:S(2)}, u32[]{:S(2)}) collective-permute-start(bf16[24,3072]{1,0:T(8,128)(2,1)S(1)} %get-tuple-element.635), channel_id=1, source_target_pairs={{32,0},{64,32},{96,64},{128,96},{160,128},{192,160},{224,192},{256... | collective-permute-start | bytes 442376 | tf_op jit(solution)/shard_map/while/body/eval_jaxpr/ppermute | solution.py:12
  827.6 14.6 collective-permute-start.1
  844.5 21.2 %collective-permute-start.1 = (bf16[24,3072]{1,0:T(8,128)(2,1)S(1)}, bf16[24,3072]{1,0:T(8,128)(2,1)S(1)}, u32[]{:S(2)}, u32[]{:S(2)}) collective-permute-start(bf16[24,3072]{1,0:T(8,128)(2,1)S(1)} %get-tuple-element.635), channel_id=1, source_target_pairs={{32,0},{64,32},{96,64},{128,96},{160,128},{192,160},{224,192},{256... | collective-permute-start | bytes 442376 | tf_op jit(solution)/shard_map/while/body/eval_jaxpr/ppermute | solution.py:12
  867.9 18.2 %collective-permute-start.1 = (bf16[24,3072]{1,0:T(8,128)(2,1)S(1)}, bf16[24,3072]{1,0:T(8,128)(2,1)S(1)}, u32[]{:S(2)}, u32[]{:S(2)}) collective-permute-start(bf16[24,3072]{1,0:T(8,128)(2,1)S(1)} %get-tuple-element.635), channel_id=1, source_target_pairs={{32,0},{64,32},{96,64},{128,96},{160,128},{192,160},{224,192},{256... | collective-permute-start | bytes 442376 | tf_op jit(solution)/shard_map/while/body/eval_jaxpr/ppermute | solution.py:12
  888.3 20.2 %collective-permute-start.1 = (bf16[24,3072]{1,0:T(8,128)(2,1)S(1)}, bf16[24,3072]{1,0:T(8,128)(2,1)S(1)}, u32[]{:S(2)}, u32[]{:S(2)}) collective-permute-start(bf16[24,3072]{1,0:T(8,128)(2,1)S(1)} %get-tuple-element.635), channel_id=1, source_target_pairs={{32,0},{64,32},{96,64},{128,96},{160,128},{192,160},{224,192},{256... | collective-permute-start | bytes 442376 | tf_op jit(solution)/shard_map/while/body/eval_jaxpr/ppermute | solution.py:12
  910.7 18.6 %collective-permute-start.1 = (bf16[24,3072]{1,0:T(8,128)(2,1)S(1)}, bf16[24,3072]{1,0:T(8,128)(2,1)S(1)}, u32[]{:S(2)}, u32[]{:S(2)}) collective-permute-start(bf16[24,3072]{1,0:T(8,128)(2,1)S(1)} %get-tuple-element.635), channel_id=1, source_target_pairs={{32,0},{64,32},{96,64},{128,96},{160,128},{192,160},{224,192},{256... | collective-permute-start | bytes 442376 | tf_op jit(solution)/shard_map/while/body/eval_jaxpr/ppermute | solution.py:12
  931.5 17.4 collective-permute-start.1
  951.2 276.5 %collective-permute-start.1 = (bf16[24,3072]{1,0:T(8,128)(2,1)S(1)}, bf16[24,3072]{1,0:T(8,128)(2,1)S(1)}, u32[]{:S(2)}, u32[]{:S(2)}) collective-permute-start(bf16[24,3072]{1,0:T(8,128)(2,1)S(1)} %get-tuple-element.635), channel_id=1, source_target_pairs={{32,0},{64,32},{96,64},{128,96},{160,128},{192,160},{224,192},{256... | collective-permute-start | bytes 442376 | tf_op jit(solution)/shard_map/while/body/eval_jaxpr/ppermute | solution.py:12
  1250.3 16.5 collective-permute-start.1
  1289.5 20.9 %collective-permute-start.1 = (bf16[24,3072]{1,0:T(8,128)(2,1)S(1)}, bf16[24,3072]{1,0:T(8,128)(2,1)S(1)}, u32[]{:S(2)}, u32[]{:S(2)}) collective-permute-start(bf16[24,3072]{1,0:T(8,128)(2,1)S(1)} %get-tuple-element.635), channel_id=1, source_target_pairs={{32,0},{64,32},{96,64},{128,96},{160,128},{192,160},{224,192},{256... | collective-permute-start | bytes 442376 | tf_op jit(solution)/shard_map/while/body/eval_jaxpr/ppermute | solution.py:12
  1333.0 14.4 collective-permute-start.1
  1370.0 13.5 collective-permute-start.1
  1406.1 17.3 collective-permute-start.1
  1446.0 10.9 collective-permute-start.1
  1459.1 25.9 %collective-permute-start.1 = (bf16[24,3072]{1,0:T(8,128)(2,1)S(1)}, bf16[24,3072]{1,0:T(8,128)(2,1)S(1)}, u32[]{:S(2)}, u32[]{:S(2)}) collective-permute-start(bf16[24,3072]{1,0:T(8,128)(2,1)S(1)} %get-tuple-element.635), channel_id=1, source_target_pairs={{32,0},{64,32},{96,64},{128,96},{160,128},{192,160},{224,192},{256... | collective-permute-start | bytes 442376 | tf_op jit(solution)/shard_map/while/body/eval_jaxpr/ppermute | solution.py:12
  1487.2 12.4 collective-permute-start.1
Sparse Core Ops, SparseCore 0:
  10.1 70.8 all-gather.4
  83.2 65.3 all-gather.6
  1502.7 295.6 all-reduce.1
where the time goes:
time: 1810 us
  waiting for transfers between devices  1080 us (60%)
  starting transfers between devices  289 us (16%)
  local copies, waits for them, and re-layouts  199 us (11%)
  other arithmetic  110 us (6%)
  matrix products  84.7 us (5%)
  loops' own time  30.9 us (2%)
    ppermute x42, waiting for transfers between devices, shifted(): return lax.ppermute(array, axis, pairs)  655 us
    psum x1, waiting for transfers between devices, per_device(): left_total = lax.psum(left_term, 'dp').astype(jnp.float32)  296 us
    ppermute x42, starting transfers between devices, shifted(): return lax.ppermute(array, axis, pairs)  289 us
    all_gather x1, waiting for transfers between devices, per_device(): lax.all_gather(left_factor[0], 'dp', axis=0, tiled=True)  67.5 us
    all_gather x1, waiting for transfers between devices, per_device(): lax.all_gather(right_factor[0], 'dp', axis=0, tiled=True)  59.8 us
    gather x6, local copies, waits for them, and re-layouts, layer_forward(): permuted = jnp.take(mixed, shuffle, axis=1)  55 us
    gather x6, local copies, waits for them, and re-layouts, layer_backward(): before = jnp.take(through, inverse, axis=1)  55 us
    dynamic_update_slice x84, other arithmetic, store_slot(): lax.dynamic_update_index_in_dim(buffer, jnp.where(is_valid, new_value, ol...  51.3 us
  transfers between devices with their start and end apart: 45, of which 37 were waited for; matrix products, arithmetic and copies ran while one was open for 5% of the time, Pallas kernels for 0%

commit v1 on v0

--- a/solution.py
+++ b/solution.py
@@ -4,6 +4,11 @@
 from jax.sharding import PartitionSpec as P
 
 epsilon = 1e-05
+
+
+def summed_here(x, name):
+    terms = lax.all_gather(x, name)
+    return jnp.sum(terms, axis=0)
 
 
 def shifted(array, axis, by):
@@ -160,7 +165,7 @@
         left_rows, right_rows, (((0,), (0,)), ((), ())), preferred_element_type=jnp.float32
     )
     left_term = left_term.astype(jnp.bfloat16)
-    left_total = lax.psum(left_term, "dp").astype(jnp.float32)
+    left_total = summed_here(left_term, "dp").astype(jnp.float32)
     share_rows = block_size // lax.axis_size("dp")
     first_row = lax.axis_index("dp") * share_rows
     left_shard = lax.dynamic_slice_in_dim(left_total, first_row, share_rows, 0)

time: 1810 us -> 1750 us (0.967)
  the two profiles are of different devices: /device:TPU:8 before, /device:TPU:1 now
where the time goes in v1:
time: 1750 us
  waiting for transfers between devices  998 us (57%)
  starting transfers between devices  298 us (17%)
  local copies, waits for them, and re-layouts  199 us (11%)
  other arithmetic  122 us (7%)
  matrix products  84.7 us (5%)
  loops' own time  30.9 us (2%)
    ppermute x42, waiting for transfers between devices, shifted(): return lax.ppermute(array, axis, pairs)  614 us
    ppermute x42, starting transfers between devices, shifted(): return lax.ppermute(array, axis, pairs)  298 us
    all_gather x1, waiting for transfers between devices, summed_here(): terms = lax.all_gather(x, name)  254 us
    all_gather x1, waiting for transfers between devices, per_device(): lax.all_gather(left_factor[0], 'dp', axis=0, tiled=True)  67.5 us
    all_gather x1, waiting for transfers between devices, per_device(): lax.all_gather(right_factor[0], 'dp', axis=0, tiled=True)  61.1 us
    gather x6, local copies, waits for them, and re-layouts, layer_backward(): before = jnp.take(through, inverse, axis=1)  55 us
    gather x6, local copies, waits for them, and re-layouts, layer_forward(): permuted = jnp.take(mixed, shuffle, axis=1)  55 us
    dynamic_update_slice x84, other arithmetic, store_slot(): lax.dynamic_update_index_in_dim(buffer, jnp.where(is_valid, new_value, ol...  51.3 us
  transfers between devices with their start and end apart: 45, of which 24 were waited for; matrix products, arithmetic and copies ran while one was open for 5% of the time, Pallas kernels for 0%

profile of v1, /device:TPU:1, one launch (start us, length us, event | category | flops | bytes accessed | tf_op | source)
XLA Modules:
  0.0 1746.1 jit_solution(14217181216083214808)
XLA Ops:
  9.5 11.8 scatter_custom_fusion
  21.3 61.1 %all-gather.7.cloned.1.call-done = bf16[1,3072,768]{2,1,0:T(8,128)(2,1)} async-done(((bf16[1,96,768]{2,1,0:T(8,128)(2,1)}), bf16[1,3072,768]{2,1,0:T(8,128)(2,1)}) %all-gather.7.cloned.1.call-update) | async-done | bytes 4718608 | tf_op jit(solution)/shard_map/all_gather | solution.py:87
  82.3 67.5 %all-gather.9.cloned.1.call-done = bf16[1,3072,768]{2,1,0:T(8,128)(2,1)} async-done(((bf16[1,96,768]{2,1,0:T(8,128)(2,1)}), bf16[1,3072,768]{2,1,0:T(8,128)(2,1)}) %all-gather.9.cloned.1.call-update) | async-done | bytes 4718608 | tf_op jit(solution)/shard_map/all_gather | solution.py:88
  152.1 506.0 %while.30 = (s32[]{:T(128)}, bf16[24,3072]{1,0:T(8,128)(2,1)S(1)}, bf16[6,24,3072]{2,1,0:T(8,128)(2,1)S(1)}, bf16[6,24,768]{1,2,0:T(8,128)(2,1)}, bf16[6,24,3072...) while((s32[]{:T(128)}, bf16[24,3072]{1,0:T(8,128)(2,1)S(1)}, ...), condition=%wide.region_4.6_spmd, body=%wide.region_0.5_spmd.sunk | while | flops 227721248 | bytes 15824611 | solution.py:151
  154.3 19.3 %conditional.4 = (bf16[24,3072]{1,0:T(8,128)(2,1)S(1)}, bf16[24,768]{0,1:T(8,128)(2,1)S(1)}) conditional(s32[]{:T(128)} %convert_element_type.99, () %tuple.71, (bf16[24,3072]{1,0:T(8,128)(2,1)S(1)}, f32[1,3072]{1,0:T(1,128)S(1)}, bf16[3072,768]{1,0:T(8,128)(2,1)}, s32[3072]{0:T(1024)S(1)}, bf16[3072,768]{1,0:T(8,128)(2,1)}) %tuple.72), branch_computations={%region_1.1_spmd, %region_2.4_spmd} | conditional | flops 227481632 | bytes 13120912 | solution.py:124
  158.1 9.2 gather_fusion.1
  180.6 19.3 %conditional.4 = (bf16[24,3072]{1,0:T(8,128)(2,1)S(1)}, bf16[24,768]{0,1:T(8,128)(2,1)S(1)}) conditional(s32[]{:T(128)} %convert_element_type.99, () %tuple.71, (bf16[24,3072]{1,0:T(8,128)(2,1)S(1)}, f32[1,3072]{1,0:T(1,128)S(1)}, bf16[3072,768]{1,0:T(8,128)(2,1)}, s32[3072]{0:T(1024)S(1)}, bf16[3072,768]{1,0:T(8,128)(2,1)}) %tuple.72), branch_computations={%region_1.1_spmd, %region_2.4_spmd} | conditional | flops 227481632 | bytes 13120912 | solution.py:124
  184.4 9.2 gather_fusion.1
  199.9 7.9 collective-permute-start
  213.4 19.3 %conditional.4 = (bf16[24,3072]{1,0:T(8,128)(2,1)S(1)}, bf16[24,768]{0,1:T(8,128)(2,1)S(1)}) conditional(s32[]{:T(128)} %convert_element_type.99, () %tuple.71, (bf16[24,3072]{1,0:T(8,128)(2,1)S(1)}, f32[1,3072]{1,0:T(1,128)S(1)}, bf16[3072,768]{1,0:T(8,128)(2,1)}, s32[3072]{0:T(1024)S(1)}, bf16[3072,768]{1,0:T(8,128)(2,1)}) %tuple.72), branch_computations={%region_1.1_spmd, %region_2.4_spmd} | conditional | flops 227481632 | bytes 13120912 | solution.py:124
  217.2 9.2 gather_fusion.1
  245.3 19.3 %conditional.4 = (bf16[24,3072]{1,0:T(8,128)(2,1)S(1)}, bf16[24,768]{0,1:T(8,128)(2,1)S(1)}) conditional(s32[]{:T(128)} %convert_element_type.99, () %tuple.71, (bf16[24,3072]{1,0:T(8,128)(2,1)S(1)}, f32[1,3072]{1,0:T(1,128)S(1)}, bf16[3072,768]{1,0:T(8,128)(2,1)}, s32[3072]{0:T(1024)S(1)}, bf16[3072,768]{1,0:T(8,128)(2,1)}) %tuple.72), branch_computations={%region_1.1_spmd, %region_2.4_spmd} | conditional | flops 227481632 | bytes 13120912 | solution.py:124
  249.0 9.2 gather_fusion.1
  276.7 19.3 %conditional.4 = (bf16[24,3072]{1,0:T(8,128)(2,1)S(1)}, bf16[24,768]{0,1:T(8,128)(2,1)S(1)}) conditional(s32[]{:T(128)} %convert_element_type.99, () %tuple.71, (bf16[24,3072]{1,0:T(8,128)(2,1)S(1)}, f32[1,3072]{1,0:T(1,128)S(1)}, bf16[3072,768]{1,0:T(8,128)(2,1)}, s32[3072]{0:T(1024)S(1)}, bf16[3072,768]{1,0:T(8,128)(2,1)}) %tuple.72), branch_computations={%region_1.1_spmd, %region_2.4_spmd} | conditional | flops 227481632 | bytes 13120912 | solution.py:124
  280.4 9.2 gather_fusion.1
  308.1 19.3 %conditional.4 = (bf16[24,3072]{1,0:T(8,128)(2,1)S(1)}, bf16[24,768]{0,1:T(8,128)(2,1)S(1)}) conditional(s32[]{:T(128)} %convert_element_type.99, () %tuple.71, (bf16[24,3072]{1,0:T(8,128)(2,1)S(1)}, f32[1,3072]{1,0:T(1,128)S(1)}, bf16[3072,768]{1,0:T(8,128)(2,1)}, s32[3072]{0:T(1024)S(1)}, bf16[3072,768]{1,0:T(8,128)(2,1)}) %tuple.72), branch_computations={%region_1.1_spmd, %region_2.4_spmd} | conditional | flops 227481632 | bytes 13120912 | solution.py:124
  311.9 9.2 gather_fusion.1
  339.6 25.7 %collective-permute-start = (bf16[24,3072]{1,0:T(8,128)(2,1)S(1)}, bf16[24,3072]{1,0:T(8,128)(2,1)S(1)}, u32[]{:S(2)}, u32[]{:S(2)}) collective-permute-start(bf16[24,3072]{1,0:T(8,128)(2,1)S(1)} %get-tuple-element.514), channel_id=1, source_target_pairs={{0,32},{32,64},{64,96},{96,128},{128,160},{160,192},{192,224},{224... | collective-permute-start | bytes 442376 | tf_op jit(solution)/shard_map/while/body/eval_jaxpr/ppermute | solution.py:17
  383.4 26.6 %collective-permute-start = (bf16[24,3072]{1,0:T(8,128)(2,1)S(1)}, bf16[24,3072]{1,0:T(8,128)(2,1)S(1)}, u32[]{:S(2)}, u32[]{:S(2)}) collective-permute-start(bf16[24,3072]{1,0:T(8,128)(2,1)S(1)} %get-tuple-element.514), channel_id=1, source_target_pairs={{0,32},{32,64},{64,96},{96,128},{128,160},{160,192},{192,224},{224... | collective-permute-start | bytes 442376 | tf_op jit(solution)/shard_map/while/body/eval_jaxpr/ppermute | solution.py:17
  428.8 20.3 %collective-permute-start = (bf16[24,3072]{1,0:T(8,128)(2,1)S(1)}, bf16[24,3072]{1,0:T(8,128)(2,1)S(1)}, u32[]{:S(2)}, u32[]{:S(2)}) collective-permute-start(bf16[24,3072]{1,0:T(8,128)(2,1)S(1)} %get-tuple-element.514), channel_id=1, source_target_pairs={{0,32},{32,64},{64,96},{96,128},{128,160},{160,192},{192,224},{224... | collective-permute-start | bytes 442376 | tf_op jit(solution)/shard_map/while/body/eval_jaxpr/ppermute | solution.py:17
  467.8 21.2 %collective-permute-start = (bf16[24,3072]{1,0:T(8,128)(2,1)S(1)}, bf16[24,3072]{1,0:T(8,128)(2,1)S(1)}, u32[]{:S(2)}, u32[]{:S(2)}) collective-permute-start(bf16[24,3072]{1,0:T(8,128)(2,1)S(1)} %get-tuple-element.514), channel_id=1, source_target_pairs={{0,32},{32,64},{64,96},{96,128},{128,160},{160,192},{192,224},{224... | collective-permute-start | bytes 442376 | tf_op jit(solution)/shard_map/while/body/eval_jaxpr/ppermute | solution.py:17
  507.7 21.3 %collective-permute-start = (bf16[24,3072]{1,0:T(8,128)(2,1)S(1)}, bf16[24,3072]{1,0:T(8,128)(2,1)S(1)}, u32[]{:S(2)}, u32[]{:S(2)}) collective-permute-start(bf16[24,3072]{1,0:T(8,128)(2,1)S(1)} %get-tuple-element.514), channel_id=1, source_target_pairs={{0,32},{32,64},{64,96},{96,128},{128,160},{160,192},{192,224},{224... | collective-permute-start | bytes 442376 | tf_op jit(solution)/shard_map/while/body/eval_jaxpr/ppermute | solution.py:17
  534.7 9.6 collective-permute-start
  550.0 21.7 %collective-permute-start = (bf16[24,3072]{1,0:T(8,128)(2,1)S(1)}, bf16[24,3072]{1,0:T(8,128)(2,1)S(1)}, u32[]{:S(2)}, u32[]{:S(2)}) collective-permute-start(bf16[24,3072]{1,0:T(8,128)(2,1)S(1)} %get-tuple-element.514), channel_id=1, source_target_pairs={{0,32},{32,64},{64,96},{96,128},{128,160},{160,192},{192,224},{224... | collective-permute-start | bytes 442376 | tf_op jit(solution)/shard_map/while/body/eval_jaxpr/ppermute | solution.py:17
  577.3 9.5 collective-permute-start
  592.5 22.7 %collective-permute-start = (bf16[24,3072]{1,0:T(8,128)(2,1)S(1)}, bf16[24,3072]{1,0:T(8,128)(2,1)S(1)}, u32[]{:S(2)}, u32[]{:S(2)}) collective-permute-start(bf16[24,3072]{1,0:T(8,128)(2,1)S(1)} %get-tuple-element.514), channel_id=1, source_target_pairs={{0,32},{32,64},{64,96},{96,128},{128,160},{160,192},{192,224},{224... | collective-permute-start | bytes 442376 | tf_op jit(solution)/shard_map/while/body/eval_jaxpr/ppermute | solution.py:17
  620.9 8.8 collective-permute-start
  635.4 19.4 %collective-permute-start = (bf16[24,3072]{1,0:T(8,128)(2,1)S(1)}, bf16[24,3072]{1,0:T(8,128)(2,1)S(1)}, u32[]{:S(2)}, u32[]{:S(2)}) collective-permute-start(bf16[24,3072]{1,0:T(8,128)(2,1)S(1)} %get-tuple-element.514), channel_id=1, source_target_pairs={{0,32},{32,64},{64,96},{96,128},{128,160},{160,192},{192,224},{224... | collective-permute-start | bytes 442376 | tf_op jit(solution)/shard_map/while/body/eval_jaxpr/ppermute | solution.py:17
  658.1 810.9 %while.31 = (s32[]{:T(128)}, bf16[24,3072]{1,0:T(8,128)(2,1)S(1)}, bf16[6,24,768]{2,1,0:T(8,128)(2,1)S(1)}, s32[21]{0:T(128)S(1)}, s32[]{:T(128)}, /*index=5*/pr...) while((s32[]{:T(128)}, bf16[24,3072]{1,0:T(8,128)(2,1)S(1)}, ...), condition=%wide.region_11.13_spmd, body=%wide.region_6.12_spmd.sunk | while | flops 227942480 | bytes 15207745 | solution.py:158
  661.7 9.9 collective-permute-done.1
  675.2 25.0 %collective-permute-done.1 = bf16[24,3072]{1,0:T(8,128)(2,1)S(1)} collective-permute-done((bf16[24,3072]{1,0:T(8,128)(2,1)S(1)}, bf16[24,3072]{1,0:T(8,128)(2,1)S(1)}, u32[]{:S(2)}, u32[]{:S(2)}) %collective-permute-start.1) | collective-permute-done | bytes 147488 | tf_op jit(solution)/shard_map/while/body/eval_jaxpr/ppermute | solution.py:17
  703.8 14.2 collective-permute-done.1
  721.5 16.4 collective-permute-done.1
  741.5 12.8 collective-permute-done.1
  757.9 20.4 %collective-permute-done.1 = bf16[24,3072]{1,0:T(8,128)(2,1)S(1)} collective-permute-done((bf16[24,3072]{1,0:T(8,128)(2,1)S(1)}, bf16[24,3072]{1,0:T(8,128)(2,1)S(1)}, u32[]{:S(2)}, u32[]{:S(2)}) %collective-permute-start.1) | collective-permute-done | bytes 147488 | tf_op jit(solution)/shard_map/while/body/eval_jaxpr/ppermute | solution.py:17
  781.9 11.2 collective-permute-done.1
  796.6 22.4 %collective-permute-done.1 = bf16[24,3072]{1,0:T(8,128)(2,1)S(1)} collective-permute-done((bf16[24,3072]{1,0:T(8,128)(2,1)S(1)}, bf16[24,3072]{1,0:T(8,128)(2,1)S(1)}, u32[]{:S(2)}, u32[]{:S(2)}) %collective-permute-start.1) | collective-permute-done | bytes 147488 | tf_op jit(solution)/shard_map/while/body/eval_jaxpr/ppermute | solution.py:17
  822.6 11.6 collective-permute-done.1
  837.7 21.7 %collective-permute-done.1 = bf16[24,3072]{1,0:T(8,128)(2,1)S(1)} collective-permute-done((bf16[24,3072]{1,0:T(8,128)(2,1)S(1)}, bf16[24,3072]{1,0:T(8,128)(2,1)S(1)}, u32[]{:S(2)}, u32[]{:S(2)}) %collective-permute-start.1) | collective-permute-done | bytes 147488 | tf_op jit(solution)/shard_map/while/body/eval_jaxpr/ppermute | solution.py:17
  863.0 11.2 collective-permute-done.1
  877.8 25.5 %collective-permute-done.1 = bf16[24,3072]{1,0:T(8,128)(2,1)S(1)} collective-permute-done((bf16[24,3072]{1,0:T(8,128)(2,1)S(1)}, bf16[24,3072]{1,0:T(8,128)(2,1)S(1)}, u32[]{:S(2)}, u32[]{:S(2)}) %collective-permute-start.1) | collective-permute-done | bytes 147488 | tf_op jit(solution)/shard_map/while/body/eval_jaxpr/ppermute | solution.py:17
  906.9 8.9 collective-permute-done.1
  919.4 29.0 %collective-permute-done.1 = bf16[24,3072]{1,0:T(8,128)(2,1)S(1)} collective-permute-done((bf16[24,3072]{1,0:T(8,128)(2,1)S(1)}, bf16[24,3072]{1,0:T(8,128)(2,1)S(1)}, u32[]{:S(2)}, u32[]{:S(2)}) %collective-permute-start.1) | collective-permute-done | bytes 147488 | tf_op jit(solution)/shard_map/while/body/eval_jaxpr/ppermute | solution.py:17
  951.9 304.7 %collective-permute-done.1 = bf16[24,3072]{1,0:T(8,128)(2,1)S(1)} collective-permute-done((bf16[24,3072]{1,0:T(8,128)(2,1)S(1)}, bf16[24,3072]{1,0:T(8,128)(2,1)S(1)}, u32[]{:S(2)}, u32[]{:S(2)}) %collective-permute-start.1) | collective-permute-done | bytes 147488 | tf_op jit(solution)/shard_map/while/body/eval_jaxpr/ppermute | solution.py:17
  1258.8 20.4 %conditional.5 = (bf16[24,3072]{1,0:T(8,128)(2,1)S(1)}) conditional(s32[]{:T(128)} %convert_element_type.100, () %tuple.74, (bf16[24,3072]{1,0:T(8,128)(2,1)S(1)}, bf16[6,24,3072]{2,1,0:T(8,128)(2,1)S(1)}, s32[]{:T(128)}, bf16[3072,768]{1,0:T(8,128)(2,1)}, s32[3072]{0:T(1024)S(1)}, /*index=5*/bf16[3072,768]{1,0:T(8,128)(2,1)}, ...), branch_computations={%region_7.8_spmd, %region_8.11_spmd} | conditional | flops 227850304 | bytes 13990880 | solution.py:140
  1264.3 9.2 gather_fusion
  1280.6 13.5 collective-permute-done.1
  1296.3 20.4 %conditional.5 = (bf16[24,3072]{1,0:T(8,128)(2,1)S(1)}) conditional(s32[]{:T(128)} %convert_element_type.100, () %tuple.74, (bf16[24,3072]{1,0:T(8,128)(2,1)S(1)}, bf16[6,24,3072]{2,1,0:T(8,128)(2,1)S(1)}, s32[]{:T(128)}, bf16[3072,768]{1,0:T(8,128)(2,1)}, s32[3072]{0:T(1024)S(1)}, /*index=5*/bf16[3072,768]{1,0:T(8,128)(2,1)}, ...), branch_computations={%region_7.8_spmd, %region_8.11_spmd} | conditional | flops 227850304 | bytes 13990880 | solution.py:140
  1301.8 9.2 gather_fusion
  1318.0 15.1 collective-permute-done.1
  1335.3 20.4 %conditional.5 = (bf16[24,3072]{1,0:T(8,128)(2,1)S(1)}) conditional(s32[]{:T(128)} %convert_element_type.100, () %tuple.74, (bf16[24,3072]{1,0:T(8,128)(2,1)S(1)}, bf16[6,24,3072]{2,1,0:T(8,128)(2,1)S(1)}, s32[]{:T(128)}, bf16[3072,768]{1,0:T(8,128)(2,1)}, s32[3072]{0:T(1024)S(1)}, /*index=5*/bf16[3072,768]{1,0:T(8,128)(2,1)}, ...), branch_computations={%region_7.8_spmd, %region_8.11_spmd} | conditional | flops 227850304 | bytes 13990880 | solution.py:140
  1340.8 9.2 gather_fusion
  1357.1 12.8 collective-permute-done.1
  1372.1 20.4 %conditional.5 = (bf16[24,3072]{1,0:T(8,128)(2,1)S(1)}) conditional(s32[]{:T(128)} %convert_element_type.100, () %tuple.74, (bf16[24,3072]{1,0:T(8,128)(2,1)S(1)}, bf16[6,24,3072]{2,1,0:T(8,128)(2,1)S(1)}, s32[]{:T(128)}, bf16[3072,768]{1,0:T(8,128)(2,1)}, s32[3072]{0:T(1024)S(1)}, /*index=5*/bf16[3072,768]{1,0:T(8,128)(2,1)}, ...), branch_computations={%region_7.8_spmd, %region_8.11_spmd} | conditional | flops 227850304 | bytes 13990880 | solution.py:140
  1377.6 9.2 gather_fusion
  1393.9 9.3 collective-permute-done.1
  1405.4 20.4 %conditional.5 = (bf16[24,3072]{1,0:T(8,128)(2,1)S(1)}) conditional(s32[]{:T(128)} %convert_element_type.100, () %tuple.74, (bf16[24,3072]{1,0:T(8,128)(2,1)S(1)}, bf16[6,24,3072]{2,1,0:T(8,128)(2,1)S(1)}, s32[]{:T(128)}, bf16[3072,768]{1,0:T(8,128)(2,1)}, s32[3072]{0:T(1024)S(1)}, /*index=5*/bf16[3072,768]{1,0:T(8,128)(2,1)}, ...), branch_computations={%region_7.8_spmd, %region_8.11_spmd} | conditional | flops 227850304 | bytes 13990880 | solution.py:140
  1410.9 9.2 gather_fusion
  1427.2 9.3 collective-permute-done.1
  1438.7 20.4 %conditional.5 = (bf16[24,3072]{1,0:T(8,128)(2,1)S(1)}) conditional(s32[]{:T(128)} %convert_element_type.100, () %tuple.74, (bf16[24,3072]{1,0:T(8,128)(2,1)S(1)}, bf16[6,24,3072]{2,1,0:T(8,128)(2,1)S(1)}, s32[]{:T(128)}, bf16[3072,768]{1,0:T(8,128)(2,1)}, s32[3072]{0:T(1024)S(1)}, /*index=5*/bf16[3072,768]{1,0:T(8,128)(2,1)}, ...), branch_computations={%region_7.8_spmd, %region_8.11_spmd} | conditional | flops 227850304 | bytes 13990880 | solution.py:140
  1444.2 9.2 gather_fusion
  1460.5 8.6 collective-permute-done.1
  1472.0 254.0 %all-gather.11.cloned.1.call-done = bf16[24576,768]{1,0:T(8,128)(2,1)} async-done(((bf16[768,768]{1,0:T(8,128)(2,1)}), bf16[24576,768]{1,0:T(8,128)(2,1)}) %all-gather.11.cloned.1.call-update) | async-done | bytes 37748752 | tf_op jit(solution)/shard_map/all_gather | solution.py:10
  1726.0 12.9 reduce_sum.41
  (547 shorter events, 357.5 us)
Async XLA Ops:
  7.2 144.9 %copy-start.1 = (s32[1,3072]{1,0:T(1,128)S(1)}, s32[1,3072]{1,0:T(1,128)}, u32[]{:S(2)}) copy-start(s32[1,3072]{1,0:T(1,128)} %param.19) | copy-start | bytes 36868
  7.2 144.9 %copy-start = (f32[1,3072]{1,0:T(1,128)S(1)}, f32[1,3072]{1,0:T(1,128)}, u32[]{:S(2)}) copy-start(f32[1,3072]{1,0:T(1,128)} %param.18) | copy-start | bytes 36868
  7.2 75.2 %all-gather.7.cloned.1.call-start = ((), (), s32[]{:S(2)}) async-start(), calls=%async_computation | async-start | bytes 4866048 | tf_op jit(solution)/shard_map/all_gather | solution.py:87
  7.9 141.9 %all-gather.9.cloned.1.call-start = ((), (), s32[]{:S(2)}) async-start(), calls=%async_computation.1 | async-start | bytes 4866048 | tf_op jit(solution)/shard_map/all_gather | solution.py:88
  8.7 1717.3 %all-gather.11.cloned.1.call-start = ((), (), s32[]{:S(2)}) async-start(), calls=%async_computation.2 | async-start | bytes 38928384 | tf_op jit(solution)/shard_map/all_gather | solution.py:10
  173.7 4.6 collective-permute-start
  199.9 11.2 collective-permute-start
  232.8 10.2 collective-permute-start
  264.6 9.8 collective-permute-start
  296.0 9.8 collective-permute-start
  327.4 9.8 collective-permute-start
  339.6 29.1 %collective-permute-start = (bf16[24,3072]{1,0:T(8,128)(2,1)S(1)}, bf16[24,3072]{1,0:T(8,128)(2,1)S(1)}, u32[]{:S(2)}, u32[]{:S(2)}) collective-permute-start(bf16[24,3072]{1,0:T(8,128)(2,1)S(1)} %get-tuple-element.514), channel_id=1, source_target_pairs={{0,32},{32,64},{64,96},{96,128},{128,160},{160,192},{192,224},{224... | collective-permute-start | bytes 442376 | tf_op jit(solution)/shard_map/while/body/eval_jaxpr/ppermute | solution.py:17
  371.0 10.0 collective-permute-start
  383.4 30.0 %collective-permute-start = (bf16[24,3072]{1,0:T(8,128)(2,1)S(1)}, bf16[24,3072]{1,0:T(8,128)(2,1)S(1)}, u32[]{:S(2)}, u32[]{:S(2)}) collective-permute-start(bf16[24,3072]{1,0:T(8,128)(2,1)S(1)} %get-tuple-element.514), channel_id=1, source_target_pairs={{0,32},{32,64},{64,96},{96,128},{128,160},{160,192},{192,224},{224... | collective-permute-start | bytes 442376 | tf_op jit(solution)/shard_map/while/body/eval_jaxpr/ppermute | solution.py:17
  415.7 10.7 collective-permute-start
  428.8 23.6 %collective-permute-start = (bf16[24,3072]{1,0:T(8,128)(2,1)S(1)}, bf16[24,3072]{1,0:T(8,128)(2,1)S(1)}, u32[]{:S(2)}, u32[]{:S(2)}) collective-permute-start(bf16[24,3072]{1,0:T(8,128)(2,1)S(1)} %get-tuple-element.514), channel_id=1, source_target_pairs={{0,32},{32,64},{64,96},{96,128},{128,160},{160,192},{192,224},{224... | collective-permute-start | bytes 442376 | tf_op jit(solution)/shard_map/while/body/eval_jaxpr/ppermute | solution.py:17
  454.7 10.7 collective-permute-start
  467.8 24.5 %collective-permute-start = (bf16[24,3072]{1,0:T(8,128)(2,1)S(1)}, bf16[24,3072]{1,0:T(8,128)(2,1)S(1)}, u32[]{:S(2)}, u32[]{:S(2)}) collective-permute-start(bf16[24,3072]{1,0:T(8,128)(2,1)S(1)} %get-tuple-element.514), channel_id=1, source_target_pairs={{0,32},{32,64},{64,96},{96,128},{128,160},{160,192},{192,224},{224... | collective-permute-start | bytes 442376 | tf_op jit(solution)/shard_map/while/body/eval_jaxpr/ppermute | solution.py:17
  494.7 10.7 collective-permute-start
  507.7 24.6 %collective-permute-start = (bf16[24,3072]{1,0:T(8,128)(2,1)S(1)}, bf16[24,3072]{1,0:T(8,128)(2,1)S(1)}, u32[]{:S(2)}, u32[]{:S(2)}) collective-permute-start(bf16[24,3072]{1,0:T(8,128)(2,1)S(1)} %get-tuple-element.514), channel_id=1, source_target_pairs={{0,32},{32,64},{64,96},{96,128},{128,160},{160,192},{192,224},{224... | collective-permute-start | bytes 442376 | tf_op jit(solution)/shard_map/while/body/eval_jaxpr/ppermute | solution.py:17
  534.7 13.0 collective-permute-start
  550.0 25.0 %collective-permute-start = (bf16[24,3072]{1,0:T(8,128)(2,1)S(1)}, bf16[24,3072]{1,0:T(8,128)(2,1)S(1)}, u32[]{:S(2)}, u32[]{:S(2)}) collective-permute-start(bf16[24,3072]{1,0:T(8,128)(2,1)S(1)} %get-tuple-element.514), channel_id=1, source_target_pairs={{0,32},{32,64},{64,96},{96,128},{128,160},{160,192},{192,224},{224... | collective-permute-start | bytes 442376 | tf_op jit(solution)/shard_map/while/body/eval_jaxpr/ppermute | solution.py:17
  577.3 12.8 collective-permute-start
  592.5 26.0 %collective-permute-start = (bf16[24,3072]{1,0:T(8,128)(2,1)S(1)}, bf16[24,3072]{1,0:T(8,128)(2,1)S(1)}, u32[]{:S(2)}, u32[]{:S(2)}) collective-permute-start(bf16[24,3072]{1,0:T(8,128)(2,1)S(1)} %get-tuple-element.514), channel_id=1, source_target_pairs={{0,32},{32,64},{64,96},{96,128},{128,160},{160,192},{192,224},{224... | collective-permute-start | bytes 442376 | tf_op jit(solution)/shard_map/while/body/eval_jaxpr/ppermute | solution.py:17
  620.9 12.2 collective-permute-start
  635.4 22.7 %collective-permute-start = (bf16[24,3072]{1,0:T(8,128)(2,1)S(1)}, bf16[24,3072]{1,0:T(8,128)(2,1)S(1)}, u32[]{:S(2)}, u32[]{:S(2)}) collective-permute-start(bf16[24,3072]{1,0:T(8,128)(2,1)S(1)} %get-tuple-element.514), channel_id=1, source_target_pairs={{0,32},{32,64},{64,96},{96,128},{128,160},{160,192},{192,224},{224... | collective-permute-start | bytes 442376 | tf_op jit(solution)/shard_map/while/body/eval_jaxpr/ppermute | solution.py:17
  660.4 11.2 collective-permute-start.1
  673.9 26.4 %collective-permute-start.1 = (bf16[24,3072]{1,0:T(8,128)(2,1)S(1)}, bf16[24,3072]{1,0:T(8,128)(2,1)S(1)}, u32[]{:S(2)}, u32[]{:S(2)}) collective-permute-start(bf16[24,3072]{1,0:T(8,128)(2,1)S(1)} %get-tuple-element.635), channel_id=1, source_target_pairs={{32,0},{64,32},{96,64},{128,96},{160,128},{192,160},{224,192},{256... | collective-permute-start | bytes 442376 | tf_op jit(solution)/shard_map/while/body/eval_jaxpr/ppermute | solution.py:17
  702.4 15.5 collective-permute-start.1
  720.2 17.8 %collective-permute-start.1 = (bf16[24,3072]{1,0:T(8,128)(2,1)S(1)}, bf16[24,3072]{1,0:T(8,128)(2,1)S(1)}, u32[]{:S(2)}, u32[]{:S(2)}) collective-permute-start(bf16[24,3072]{1,0:T(8,128)(2,1)S(1)} %get-tuple-element.635), channel_id=1, source_target_pairs={{32,0},{64,32},{96,64},{128,96},{160,128},{192,160},{224,192},{256... | collective-permute-start | bytes 442376 | tf_op jit(solution)/shard_map/while/body/eval_jaxpr/ppermute | solution.py:17
  740.2 14.2 collective-permute-start.1
  756.6 21.7 %collective-permute-start.1 = (bf16[24,3072]{1,0:T(8,128)(2,1)S(1)}, bf16[24,3072]{1,0:T(8,128)(2,1)S(1)}, u32[]{:S(2)}, u32[]{:S(2)}) collective-permute-start(bf16[24,3072]{1,0:T(8,128)(2,1)S(1)} %get-tuple-element.635), channel_id=1, source_target_pairs={{32,0},{64,32},{96,64},{128,96},{160,128},{192,160},{224,192},{256... | collective-permute-start | bytes 442376 | tf_op jit(solution)/shard_map/while/body/eval_jaxpr/ppermute | solution.py:17
  780.5 12.5 collective-permute-start.1
  795.3 23.8 %collective-permute-start.1 = (bf16[24,3072]{1,0:T(8,128)(2,1)S(1)}, bf16[24,3072]{1,0:T(8,128)(2,1)S(1)}, u32[]{:S(2)}, u32[]{:S(2)}) collective-permute-start(bf16[24,3072]{1,0:T(8,128)(2,1)S(1)} %get-tuple-element.635), channel_id=1, source_target_pairs={{32,0},{64,32},{96,64},{128,96},{160,128},{192,160},{224,192},{256... | collective-permute-start | bytes 442376 | tf_op jit(solution)/shard_map/while/body/eval_jaxpr/ppermute | solution.py:17
  821.2 12.9 collective-permute-start.1
  836.4 23.1 %collective-permute-start.1 = (bf16[24,3072]{1,0:T(8,128)(2,1)S(1)}, bf16[24,3072]{1,0:T(8,128)(2,1)S(1)}, u32[]{:S(2)}, u32[]{:S(2)}) collective-permute-start(bf16[24,3072]{1,0:T(8,128)(2,1)S(1)} %get-tuple-element.635), channel_id=1, source_target_pairs={{32,0},{64,32},{96,64},{128,96},{160,128},{192,160},{224,192},{256... | collective-permute-start | bytes 442376 | tf_op jit(solution)/shard_map/while/body/eval_jaxpr/ppermute | solution.py:17
  861.7 12.5 collective-permute-start.1
  876.4 26.9 %collective-permute-start.1 = (bf16[24,3072]{1,0:T(8,128)(2,1)S(1)}, bf16[24,3072]{1,0:T(8,128)(2,1)S(1)}, u32[]{:S(2)}, u32[]{:S(2)}) collective-permute-start(bf16[24,3072]{1,0:T(8,128)(2,1)S(1)} %get-tuple-element.635), channel_id=1, source_target_pairs={{32,0},{64,32},{96,64},{128,96},{160,128},{192,160},{224,192},{256... | collective-permute-start | bytes 442376 | tf_op jit(solution)/shard_map/while/body/eval_jaxpr/ppermute | solution.py:17
  905.5 10.3 collective-permute-start.1
  918.0 30.3 %collective-permute-start.1 = (bf16[24,3072]{1,0:T(8,128)(2,1)S(1)}, bf16[24,3072]{1,0:T(8,128)(2,1)S(1)}, u32[]{:S(2)}, u32[]{:S(2)}) collective-permute-start(bf16[24,3072]{1,0:T(8,128)(2,1)S(1)} %get-tuple-element.635), channel_id=1, source_target_pairs={{32,0},{64,32},{96,64},{128,96},{160,128},{192,160},{224,192},{256... | collective-permute-start | bytes 442376 | tf_op jit(solution)/shard_map/while/body/eval_jaxpr/ppermute | solution.py:17
  950.6 306.0 %collective-permute-start.1 = (bf16[24,3072]{1,0:T(8,128)(2,1)S(1)}, bf16[24,3072]{1,0:T(8,128)(2,1)S(1)}, u32[]{:S(2)}, u32[]{:S(2)}) collective-permute-start(bf16[24,3072]{1,0:T(8,128)(2,1)S(1)} %get-tuple-element.635), channel_id=1, source_target_pairs={{32,0},{64,32},{96,64},{128,96},{160,128},{192,160},{224,192},{256... | collective-permute-start | bytes 442376 | tf_op jit(solution)/shard_map/while/body/eval_jaxpr/ppermute | solution.py:17
  1279.2 14.8 collective-permute-start.1
  1316.7 16.4 collective-permute-start.1
  1355.7 14.2 collective-permute-start.1
  1392.5 10.7 collective-permute-start.1
  1425.8 10.7 collective-permute-start.1
  1459.1 9.9 collective-permute-start.1
Sparse Core Ops, SparseCore 0:
  10.1 72.1 all-gather.6
  84.5 65.2 all-gather.8
  1472.1 253.8 all-gather.10
